TPU v7x, 256 devices: a whole 4x4x8 slice. The times are simulated.
256 devices in a mesh: row: 8 (over y, x_lo), col: 32 (over x_hi, z, core).
Axes of the slice: x: 4 (x_hi: 2, x_lo: 2; x = x_hi * 2 + x_lo), y: 4, z: 8, core: 2. Of those that a mesh axis runs over, the one named last changes fastest.
Arguments:
- features: bfloat16 [32768, 768], P(('row', 'col')), may hold values from -6 to 6
- cotangent: bfloat16 [32768, 768], P(('row', 'col')), may hold values from -6 to 6
- w_self: bfloat16 [768, 768], replicated, may hold values from -0.21875 to 0.21875
- w_neigh: bfloat16 [768, 768], replicated, may hold values from -0.21875 to 0.21875
- degree: int32 [32768], P(('row', 'col')), may hold values from 16 to 64
- block_cols: int32 [8, 32, 32, 4], P('row', 'col'), may hold values from 0 to 7, as said below
- block_count: int32 [8, 32, 32], P('row', 'col'), may hold values from 0 to 4, as said below
- blocks: bfloat16 [8, 32, 32, 4, 128, 128], P('row', 'col'), may hold values from 0 to 1, as said below
Outputs:
- output: bfloat16 [32768, 768], P(('row', 'col'))
- grad_features: bfloat16 [32768, 768], P(('row', 'col'))
- grad_w_self: float32 [768, 768], replicated
- grad_w_neigh: float32 [768, 768], replicated
Inputs may be any that keep to these rules, and one draw needn't show every extreme that they name: `block_cols`: within one block row of a tile the 4 block columns are distinct. The live slots of a block row are its first block_count ones. `blocks`: every entry of a slot at or past its block row's live count is zero.
All inputs are finite; a program needn't handle non-finite values.
Results may differ from a plain program's by a relative error of at most 0.015.
Values may be sent and summed in bfloat16 or wider, within the bound.
No kernel may reach another device: no remote copies, remote signals or barrier semaphores. Data moves between devices by JAX's collectives and lax.ppermute only.
A program may use at most 128 MiB of HBM per device.

v0:
```python
import jax
import jax.numpy as jnp
from jax import lax
from jax.sharding import PartitionSpec as P


def silu_slope(hidden):
    sigmoid_value = jax.nn.sigmoid(hidden)
    return sigmoid_value * (1.0 + hidden * (1.0 - sigmoid_value))


def per_device(features, cotangent, w_self, w_neigh, degree, block_cols, block_count, blocks):
    node_rows, feature_width = features.shape
    block_size = blocks.shape[-1]
    block_list = block_cols[0, 0]
    row_loads = block_count[0, 0]
    tile_blocks = blocks[0, 0]
    tile_rows, slot_count = block_list.shape
    source_count = lax.axis_size("row") * node_rows // block_size
    source_iota = jnp.arange(source_count, dtype=jnp.int32)
    slot_iota = jnp.arange(slot_count, dtype=jnp.int32)
    live_slots = slot_iota[None, :] < row_loads[:, None]
    placement = (
        (block_list[:, :, None] == source_iota[None, None, :]) & live_slots[:, :, None]
    ).astype(jnp.bfloat16)
    dense_tile = jnp.einsum(
        "rks,rkab->rasb", placement, tile_blocks, preferred_element_type=jnp.bfloat16
    )
    dense_tile = dense_tile.reshape(tile_rows * block_size, source_count * block_size)
    sources = lax.all_gather(features, "row", axis=0, tiled=True)
    summed = lax.psum_scatter(
        jnp.dot(dense_tile, sources, preferred_element_type=jnp.float32),
        "col",
        scatter_dimension=0,
        tiled=True,
    )
    degree_f = degree.astype(jnp.float32)[:, None]
    aggregate = (summed / degree_f).astype(jnp.bfloat16)
    hidden = jnp.dot(features, w_self, preferred_element_type=jnp.float32) + jnp.dot(
        aggregate, w_neigh, preferred_element_type=jnp.float32
    )
    output = jax.nn.silu(hidden).astype(jnp.bfloat16)
    hidden_grad = (cotangent.astype(jnp.float32) * silu_slope(hidden)).astype(jnp.bfloat16)
    grad_scale = float(node_rows * lax.axis_size("row") * lax.axis_size("col")) ** (-0.5)
    across_rows = (((0,), (0,)), ((), ()))
    term_self = (
        lax.dot_general(features, hidden_grad, across_rows, preferred_element_type=jnp.float32)
        * grad_scale
    )
    term_neigh = (
        lax.dot_general(aggregate, hidden_grad, across_rows, preferred_element_type=jnp.float32)
        * grad_scale
    )
    against_cols = (((1,), (1,)), ((), ()))
    neigh_grad = (
        lax.dot_general(hidden_grad, w_neigh, against_cols, preferred_element_type=jnp.float32)
        / degree_f
    ).astype(jnp.bfloat16)
    targets = lax.all_gather(neigh_grad, "col", axis=0, tiled=True)
    gathered = lax.dot_general(dense_tile, targets, across_rows, preferred_element_type=jnp.float32)
    source_part = lax.psum_scatter(
        gathered.astype(jnp.bfloat16), "row", scatter_dimension=0, tiled=True
    ).astype(jnp.float32)
    grad_features = (
        lax.dot_general(hidden_grad, w_self, against_cols, preferred_element_type=jnp.float32)
        + source_part
    ).astype(jnp.bfloat16)
    grad_w_self, grad_w_neigh = lax.psum((term_self, term_neigh), ("row", "col"))
    return (output, grad_features, grad_w_self, grad_w_neigh)


def solution(mesh):
    placed = (
        P(("row", "col"), None),
        P(("row", "col"), None),
        P(),
        P(),
        P(("row", "col")),
        P("row", "col", None, None),
        P("row", "col", None),
        P("row", "col", None, None, None, None),
    )
    return jax.shard_map(
        per_device,
        mesh=mesh,
        in_specs=placed,
        out_specs=(P(("row", "col"), None), P(("row", "col"), None), P(), P()),
        check_vma=False,
    )
```

profile of v0, /device:TPU:4, one launch (start us, length us, event | category | flops | bytes accessed | tf_op | source)
XLA Modules:
  0.0 674.5 jit_solution(432152945170127482)
XLA Ops:
  7.2 0.0 copy-start
  7.2 0.0 all-gather.3.cloned.1.call-start
  7.2 0.7 all-gather.3.cloned.1.call-update
  7.9 0.0 reduce-scatter.3.cloned.1.call-start
  8.0 0.8 copy.12
  8.7 0.7 iota_compare_fusion.1
  9.5 8.8 %fusion.6 = bf16[32,8,128,128]{3,1,2,0:T(8,128)(2,1)} fusion(bf16[32,4,128,128]{3,2,1,0:T(8,128)(2,1)} %bitcast.34, s32[32,4]{1,0:T(8,128)S(1)} %copy.12, pred[32,4]{1,0:T(8,128)(4,1)S(1)} %iota_compare_fusion.1), kind=kOutput, calls=%fused_computation.6 | convolution fusion | flops 33556480 | bytes 12583552 | tf_op jit(solution)/shard_map/rks,rkab->rasb/dot_general | solution.py:26
  18.2 40.3 %all-gather.3.cloned.1.call-done = bf16[1024,768]{1,0:T(8,128)(2,1)} async-done(((bf16[128,768]{1,0:T(8,128)(2,1)}), bf16[1024,768]{1,0:T(8,128)(2,1)}) %all-gather.3.cloned.1.call-update) | async-done | bytes 1572880 | tf_op jit(solution)/shard_map/all_gather | solution.py:30
  58.5 12.2 %fusion.2 = f32[4096,768]{1,0:T(8,128)} fusion(bf16[1024,768]{1,0:T(8,128)(2,1)} %all-gather.3.cloned.1.call-done, bf16[512,8,8,128]{3,2,1,0:T(8,128)(2,1)} %bitcast.32), kind=kOutput, calls=%fused_computation.2 | convolution fusion | flops 6442450944 | bytes 22544384 | tf_op jit(solution)/shard_map/dot_general | solution.py:32
  70.8 0.0 reduce-scatter.3.cloned.1.call-update
  70.8 0.0 all-gather.5.cloned.1.call-start
  70.9 0.6 copy-done.5
  71.4 0.6 copy-done.1
  72.1 0.0 copy-done.2
  72.1 0.3 fusion.18
  72.4 169.3 %reduce-scatter.3.cloned.1.call-done = f32[128,768]{1,0:T(8,128)} async-done(((f32[4096,768]{1,0:T(8,128)}), f32[128,768]{1,0:T(8,128)}) %reduce-scatter.3.cloned.1.call-update) | async-done | bytes 393232 | tf_op jit(solution)/shard_map/reduce_scatter | solution.py:31
  241.7 2.1 multiply_convert_fusion
  243.8 1.2 fusion.12
  245.0 0.0 all-gather.5.cloned.1.call-update
  245.0 0.0 all-reduce.3.cloned.1.call-start
  245.1 1.9 multiply_bitcast_fusion
  247.0 2.0 convolution_multiply_fusion
  249.0 0.0 all-reduce.3.cloned.1.call-update
  249.0 0.0 reduce-scatter.5.cloned.1.call-start
  249.0 89.1 %all-gather.5.cloned.1.call-done = bf16[4096,768]{1,0:T(8,128)(2,1)} async-done(((bf16[128,768]{1,0:T(8,128)(2,1)}), bf16[4096,768]{1,0:T(8,128)(2,1)}) %all-gather.5.cloned.1.call-update) | async-done | bytes 6291472 | tf_op jit(solution)/shard_map/all_gather | solution.py:59
  338.1 11.7 %fusion.8 = bf16[1024,768]{1,0:T(8,128)(2,1)} fusion(bf16[4096,768]{1,0:T(8,128)(2,1)} %all-gather.5.cloned.1.call-done, bf16[512,8,8,128]{3,2,1,0:T(8,128)(2,1)} %bitcast.33), kind=kOutput, calls=%fused_computation.10 | convolution fusion | flops 6443237376 | bytes 16252928 | tf_op jit(solution)/shard_map/dot_general | solution.py:60
  349.8 0.0 reduce-scatter.5.cloned.1.call-update
  349.8 264.9 %all-reduce.3.cloned.1.call-done = (f32[768,768]{0,1:T(8,128)}, f32[768,768]{1,0:T(8,128)}) async-done(((f32[768,768]{0,1:T(8,128)}, f32[768,768]{1,0:T(8,128)}), (f32[768,768]{0,1:T(8,128)}, f32[768,768]{1,0:T(8,128)})) %all-reduce.3.cloned.1.call-update) | async-done | bytes 4718608 | tf_op jit(solution)/shard_map/psum | solution.py:68
  614.7 3.0 copy.14
  617.8 44.8 %reduce-scatter.5.cloned.1.call-done = bf16[128,768]{1,0:T(8,128)(2,1)} async-done(((bf16[1024,768]{1,0:T(8,128)(2,1)}), bf16[128,768]{1,0:T(8,128)(2,1)}) %reduce-scatter.5.cloned.1.call-update) | async-done | bytes 196624 | tf_op jit(solution)/shard_map/reduce_scatter | solution.py:61
  662.6 2.1 fusion.11
  664.7 3.2 copy.31
  (9 shorter events, 0.0 us)
Async XLA Ops:
  7.2 234.5 %copy-start = (bf16[768,768]{1,0:T(8,128)(2,1)S(1)}, bf16[768,768]{1,0:T(8,128)(2,1)}, u32[]{:S(2)}) copy-start(bf16[768,768]{1,0:T(8,128)(2,1)} %param.11) | copy-start | bytes 3538948
  7.2 51.3 %all-gather.3.cloned.1.call-start = ((), (), s32[]{:S(2)}) async-start(), calls=%async_computation.2 | async-start | bytes 1769472 | tf_op jit(solution)/shard_map/all_gather | solution.py:30
  7.9 233.8 %reduce-scatter.3.cloned.1.call-start = ((), (), s32[]{:S(2)}) async-start(), calls=%async_computation.3 | async-start | bytes 12976128 | tf_op jit(solution)/shard_map/reduce_scatter | solution.py:31
  70.8 0.7 copy-start.5
  70.8 1.3 copy-start.1
  70.8 1.3 copy-start.2
  70.8 170.9 %copy-start.4 = (bf16[128,768]{1,0:T(8,128)(2,1)S(1)}, bf16[128,768]{1,0:T(8,128)(2,1)}, u32[]{:S(2)}) copy-start(bf16[128,768]{1,0:T(8,128)(2,1)} %param.9) | copy-start | bytes 589828
  70.8 267.3 %all-gather.5.cloned.1.call-start = ((), (), s32[]{:S(2)}) async-start(), calls=%async_computation.4 | async-start | bytes 6488064 | tf_op jit(solution)/shard_map/all_gather | solution.py:59
  243.8 3.2 copy-start.3
  245.0 369.7 %all-reduce.3.cloned.1.call-start = ((), (), s32[]{:S(2)}) async-start(), calls=%async_computation.6 | async-start | bytes 9437184 | tf_op jit(solution)/shard_map/psum | solution.py:68
  249.0 413.6 %reduce-scatter.5.cloned.1.call-start = ((), (), s32[]{:S(2)}) async-start(), calls=%async_computation.5 | async-start | bytes 1769472 | tf_op jit(solution)/shard_map/reduce_scatter | solution.py:61
Sparse Core Ops, SparseCore 0:
  9.8 48.6 all-gather.2
  70.9 170.6 reduce-scatter.2
  245.2 92.8 all-gather.4
  344.1 270.5 all-reduce.2
  617.3 45.2 reduce-scatter.4
where the time goes:
time: 675 us; the launch traced here: 674 us
  waiting for transfers between devices  609 us (90%)
  matrix products  42.4 us (6%)
  between operations  13.8 us (2%)
  local copies, waits for them, and re-layouts  8.25 us (1%)
    psum x1, waiting for transfers between devices, per_device(): lax.psum((term_self, term_neigh), ('row', 'col'))  265 us
    reduce_scatter x1, waiting for transfers between devices, per_device(): lax.psum_scatter(jnp.dot(dense_tile, sources, preferred_element_type=jnp....  169 us
    all_gather x1, waiting for transfers between devices, per_device(): targets = lax.all_gather(neigh_grad, 'col', axis=0, tiled=True)  89.1 us
    reduce_scatter x1, waiting for transfers between devices, per_device(): lax.psum_scatter(gathered.astype(jnp.bfloat16), 'row', scatter_dimension=...  44.8 us
    all_gather x1, waiting for transfers between devices, per_device(): sources = lax.all_gather(features, 'row', axis=0, tiled=True)  40.3 us
  transfers between devices with their start and end apart: 5, of which 5 were waited for; matrix products, arithmetic and copies ran while one was open for 4% of the time, Pallas kernels for 0%

commit v1 on v0

--- a/solution.py
+++ b/solution.py
@@ -56,7 +56,10 @@
         lax.dot_general(hidden_grad, w_neigh, against_cols, preferred_element_type=jnp.float32)
         / degree_f
     ).astype(jnp.bfloat16)
-    targets = lax.all_gather(neigh_grad, "col", axis=0, tiled=True)
+    size = lax.axis_size("col")
+    shards = jnp.stack([neigh_grad for _ in range(size)])
+    shards = lax.all_to_all(shards, "col", split_axis=0, concat_axis=0)
+    targets = jnp.concatenate(shards, axis=0)
     gathered = lax.dot_general(dense_tile, targets, across_rows, preferred_element_type=jnp.float32)
     source_part = lax.psum_scatter(
         gathered.astype(jnp.bfloat16), "row", scatter_dimension=0, tiled=True

time: 675 us -> 651 us (0.964)
  waiting for transfers between devices: 609 us -> 573 us
  starting transfers between devices: 0.2 us -> 9.39 us
    all_to_all x0 -> x1, waiting for transfers between devices: none -> 148 us  [per_device(): shards = lax.all_to_all(shards, 'col', split_axis=0, concat_axis=0)]
    psum x1, waiting for transfers between devices: 265 us -> 169 us  [per_device(): lax.psum((term_self, term_neigh), ('row', 'col'))]
    all_gather x1 -> x0, waiting for transfers between devices: 89.1 us -> none  [per_device(): targets = lax.all_gather(neigh_grad, 'col', axis=0, tiled=True)]
    all_to_all x0 -> x1, starting transfers between devices: none -> 9.05 us  [per_device(): shards = lax.all_to_all(shards, 'col', split_axis=0, concat_axis=0)]
where the time goes in v1:
time: 651 us; the launch traced here: 650 us
  waiting for transfers between devices  573 us (88%)
  matrix products  41.7 us (6%)
  between operations  13.8 us (2%)
  local copies, waits for them, and re-layouts  11.7 us (2%)
  starting transfers between devices  9.39 us (1%)
    psum x1, waiting for transfers between devices, per_device(): lax.psum((term_self, term_neigh), ('row', 'col'))  169 us
    reduce_scatter x1, waiting for transfers between devices, per_device(): lax.psum_scatter(jnp.dot(dense_tile, sources, preferred_element_type=jnp....  169 us
    all_to_all x1, waiting for transfers between devices, per_device(): shards = lax.all_to_all(shards, 'col', split_axis=0, concat_axis=0)  148 us
    reduce_scatter x1, waiting for transfers between devices, per_device(): lax.psum_scatter(gathered.astype(jnp.bfloat16), 'row', scatter_dimension=...  44.9 us
    all_gather x1, waiting for transfers between devices, per_device(): sources = lax.all_gather(features, 'row', axis=0, tiled=True)  40.3 us
  transfers between devices with their start and end apart: 5, of which 5 were waited for; matrix products, arithmetic and copies ran while one was open for 4% of the time, Pallas kernels for 0%

profile of v1, /device:TPU:4, one launch (start us, length us, event | category | flops | bytes accessed | tf_op | source)
XLA Modules:
  0.0 650.2 jit_solution(154391257745947364)
XLA Ops:
  7.2 0.0 copy-start
  7.2 0.0 all-gather.2.cloned.1.call-start
  7.2 0.7 all-gather.2.cloned.1.call-update
  7.9 0.0 reduce-scatter.3.cloned.1.call-start
  8.0 0.8 copy.12
  8.7 0.7 iota_compare_fusion.1
  9.5 8.8 %fusion.6 = bf16[32,8,128,128]{3,1,2,0:T(8,128)(2,1)} fusion(bf16[32,4,128,128]{3,2,1,0:T(8,128)(2,1)} %bitcast.35, s32[32,4]{1,0:T(8,128)S(1)} %copy.12, pred[32,4]{1,0:T(8,128)(4,1)S(1)} %iota_compare_fusion.1), kind=kOutput, calls=%fused_computation.6 | convolution fusion | flops 33556480 | bytes 12583552 | tf_op jit(solution)/shard_map/rks,rkab->rasb/dot_general | solution.py:26
  18.2 40.3 %all-gather.2.cloned.1.call-done = bf16[1024,768]{1,0:T(8,128)(2,1)} async-done(((bf16[128,768]{1,0:T(8,128)(2,1)}), bf16[1024,768]{1,0:T(8,128)(2,1)}) %all-gather.2.cloned.1.call-update) | async-done | bytes 1572880 | tf_op jit(solution)/shard_map/all_gather | solution.py:30
  58.5 12.2 %fusion.2 = f32[4096,768]{1,0:T(8,128)} fusion(bf16[1024,768]{1,0:T(8,128)(2,1)} %all-gather.2.cloned.1.call-done, bf16[512,8,8,128]{3,2,1,0:T(8,128)(2,1)} %bitcast.33), kind=kOutput, calls=%fused_computation.2 | convolution fusion | flops 6442450944 | bytes 22544384 | tf_op jit(solution)/shard_map/dot_general | solution.py:32
  70.8 0.0 reduce-scatter.3.cloned.1.call-update
  70.8 0.6 copy-done.5
  71.4 0.6 copy-done.1
  72.1 0.0 copy-done.2
  72.1 0.3 fusion.18
  72.4 169.3 %reduce-scatter.3.cloned.1.call-done = f32[128,768]{1,0:T(8,128)} async-done(((f32[4096,768]{1,0:T(8,128)}), f32[128,768]{1,0:T(8,128)}) %reduce-scatter.3.cloned.1.call-update) | async-done | bytes 393232 | tf_op jit(solution)/shard_map/reduce_scatter | solution.py:31
  241.7 2.1 multiply_convert_fusion
  243.9 0.5 fusion.12
  244.4 3.4 stack.2
  247.8 9.1 %all-to-all-start = ((bf16[32,128,768]{2,1,0:T(8,128)(2,1)}), bf16[32,128,768]{2,1,0:T(8,128)(2,1)}, u32[]{:S(2)}, u32[]{:S(2)}) async-start(bf16[32,128,768]{2,1,0:T(8,128)(2,1)} %stack.2), calls=%async_computation.1 | async-start | bytes 12582912 | tf_op jit(solution)/shard_map/all_to_all | solution.py:61
  256.8 0.0 all-reduce.3.cloned.1.call-start
  256.9 1.9 multiply_bitcast_fusion
  258.8 2.0 convolution_multiply_fusion
  260.8 0.0 all-reduce.3.cloned.1.call-update
  260.8 0.2 reduce-scatter.5.cloned.1.call-start
  261.0 148.3 %all-to-all-done = bf16[32,128,768]{2,1,0:T(8,128)(2,1)} async-done(((bf16[32,128,768]{2,1,0:T(8,128)(2,1)}), bf16[32,128,768]{2,1,0:T(8,128)(2,1)}, u32[]{:S(2)}, u32[]{:S(2)}) %all-to-all-start) | async-done | bytes 6291488 | tf_op jit(solution)/shard_map/all_to_all | solution.py:61
  409.3 11.7 %fusion.8 = bf16[1024,768]{1,0:T(8,128)(2,1)} fusion(bf16[4096,768]{1,0:T(8,128)(2,1)} %bitcast.6, bf16[512,8,8,128]{3,2,1,0:T(8,128)(2,1)} %bitcast.34), kind=kOutput, calls=%fused_computation.10 | convolution fusion | flops 6443237376 | bytes 16252928 | tf_op jit(solution)/shard_map/dot_general | solution.py:63
  421.0 0.0 reduce-scatter.5.cloned.1.call-update
  421.0 169.4 %all-reduce.3.cloned.1.call-done = (f32[768,768]{0,1:T(8,128)}, f32[768,768]{1,0:T(8,128)}) async-done(((f32[768,768]{0,1:T(8,128)}, f32[768,768]{1,0:T(8,128)}), (f32[768,768]{0,1:T(8,128)}, f32[768,768]{1,0:T(8,128)})) %all-reduce.3.cloned.1.call-update) | async-done | bytes 4718608 | tf_op jit(solution)/shard_map/psum | solution.py:71
  590.4 3.0 copy.14
  593.5 44.9 %reduce-scatter.5.cloned.1.call-done = bf16[128,768]{1,0:T(8,128)(2,1)} async-done(((bf16[1024,768]{1,0:T(8,128)(2,1)}), bf16[128,768]{1,0:T(8,128)(2,1)}) %reduce-scatter.5.cloned.1.call-update) | async-done | bytes 196624 | tf_op jit(solution)/shard_map/reduce_scatter | solution.py:64
  638.3 2.1 fusion.11
  640.5 3.2 copy.31
  (9 shorter events, 0.0 us)
Async XLA Ops:
  7.2 234.6 %copy-start = (bf16[768,768]{1,0:T(8,128)(2,1)S(1)}, bf16[768,768]{1,0:T(8,128)(2,1)}, u32[]{:S(2)}) copy-start(bf16[768,768]{1,0:T(8,128)(2,1)} %param.11) | copy-start | bytes 3538948
  7.2 51.3 %all-gather.2.cloned.1.call-start = ((), (), s32[]{:S(2)}) async-start(), calls=%async_computation.3 | async-start | bytes 1769472 | tf_op jit(solution)/shard_map/all_gather | solution.py:30
  7.9 233.8 %reduce-scatter.3.cloned.1.call-start = ((), (), s32[]{:S(2)}) async-start(), calls=%async_computation.4 | async-start | bytes 12976128 | tf_op jit(solution)/shard_map/reduce_scatter | solution.py:31
  70.8 0.7 copy-start.5
  70.8 1.3 copy-start.1
  70.8 1.3 copy-start.2
  70.8 171.0 %copy-start.4 = (bf16[128,768]{1,0:T(8,128)(2,1)S(1)}, bf16[128,768]{1,0:T(8,128)(2,1)}, u32[]{:S(2)}) copy-start(bf16[128,768]{1,0:T(8,128)(2,1)} %param.9) | copy-start | bytes 589828
  247.8 161.6 %all-to-all-start = ((bf16[32,128,768]{2,1,0:T(8,128)(2,1)}), bf16[32,128,768]{2,1,0:T(8,128)(2,1)}, u32[]{:S(2)}, u32[]{:S(2)}) async-start(bf16[32,128,768]{2,1,0:T(8,128)(2,1)} %stack.2), calls=%async_computation.1 | async-start | bytes 12582912 | tf_op jit(solution)/shard_map/all_to_all | solution.py:61
  256.8 2.0 copy-start.3
  256.8 333.6 %all-reduce.3.cloned.1.call-start = ((), (), s32[]{:S(2)}) async-start(), calls=%async_computation.6 | async-start | bytes 9437184 | tf_op jit(solution)/shard_map/psum | solution.py:71
  260.8 377.5 %reduce-scatter.5.cloned.1.call-start = ((), (), s32[]{:S(2)}) async-start(), calls=%async_computation.5 | async-start | bytes 1769472 | tf_op jit(solution)/shard_map/reduce_scatter | solution.py:64
Sparse Core Ops, SparseCore 0:
  9.8 48.6 all-gather.1
  70.9 170.7 reduce-scatter.2
  263.8 326.5 all-reduce.2
  593.0 45.2 reduce-scatter.4
